TPU v7x, 128 devices: a whole 4x4x4 slice. The times are simulated.
128 devices in a mesh: doc: 8 (over x, core), term: 16 (over z, y).
Axes of the slice: x: 4, y: 4, z: 4, core: 2. Of those that a mesh axis runs over, the one named last changes fastest.
Arguments:
- query_states: bfloat16 [512, 32, 768], P('doc'), may hold values from -6 to 6
- token_ids: int32 [512, 32], P('doc'), may hold values from 0 to 30521, as said below
- transform_weight: bfloat16 [768, 768], replicated, may hold values from -0.21875 to 0.21875
- transform_bias: float32 [768], replicated, may hold values from -3 to 3
- norm_gain: float32 [768], replicated, may hold values from 0.5 to 1.5
- norm_bias: float32 [768], replicated, may hold values from -3 to 3
- decoder_weight: bfloat16 [768, 30720], P(None, 'term'), may hold values from -0.21875 to 0.21875
- decoder_bias: float32 [30720], P('term'), may hold values from -2.5 to 0.5
- candidates: int32 [512, 32], P('doc'), may hold values from 0 to 127, all different within a row; in each aligned block of 64 rows (0 to 63, 64 to 127, ...) at most 32 rows name the same one
- occupancy: int32 [128, 240], P('doc', 'term'), may hold values 0 or 1
- doc_blocks: bfloat16 [128, 240, 128, 128], P('doc', 'term'), may hold values from -0.046875 to 0.046875
Outputs:
- query_weights: bfloat16 [512, 30720], P('doc', 'term')
- scores: float32 [512, 32, 128], P('doc', None, 'term')
Inputs may be any that keep to these rules, and one draw needn't show every extreme that they name: `token_ids`: id 0 marks padding: a query has non-zero ids at its first positions, at least 8 of them, and 0 after them. `candidates`: A query names 32 different tiles; among the 64 queries of one doc index no tile is named by more than 32 of them.
All inputs are finite; a program needn't handle non-finite values. No bound on the sum of `occupancy` on one device may be relied on, other than what follows from the above.
Results may differ from a plain program's by a relative error of at most 0.0041.
Values may be sent and summed in bfloat16 or wider, within the bound.
A program may use at most 128 MiB of HBM per device.

v0:
```python
import jax
import jax.numpy as jnp
from jax import lax
from jax.sharding import PartitionSpec as P

VOCAB = 30522
MOST = 32


def tile_ranks(cand_rows, tile_total):
    tile_index = lax.iota(jnp.int32, tile_total)
    tile_hits = jnp.sum((cand_rows[..., None] == tile_index).astype(jnp.int32), axis=-2)
    tile_before = jnp.cumsum(tile_hits, axis=-2) - tile_hits
    return (tile_hits, tile_before)


def slot_sources(hits_by_tile, before_by_tile, capacity):
    row_total = hits_by_tile.shape[-1]
    slot_index = lax.iota(jnp.int32, capacity)
    chosen = (hits_by_tile[..., None, :] > 0) & (
        before_by_tile[..., None, :] == slot_index[:, None]
    )
    source_row = jnp.sum(jnp.where(chosen, lax.iota(jnp.int32, row_total), 0), axis=-1)
    return (source_row, jnp.any(chosen, axis=-1))


def body(
    query_states,
    token_ids,
    transform_weight,
    transform_bias,
    norm_gain,
    norm_bias,
    decoder_weight,
    decoder_bias,
    candidates,
    occupancy,
    doc_blocks,
):
    query_count, query_length, model_width = query_states.shape
    vocab_local = decoder_weight.shape[1]
    tile_local, blocks_local, tile_docs, block_terms = doc_blocks.shape
    cand_count = candidates.shape[1]
    term_index = lax.axis_index("term")
    doc_index = lax.axis_index("doc")
    doc_count = lax.axis_size("doc")
    term_count = lax.axis_size("term")
    tile_total = doc_count * tile_local
    hidden = (
        jnp.dot(
            query_states.reshape(query_count * query_length, model_width),
            transform_weight,
            preferred_element_type=jnp.float32,
        )
        + transform_bias
    )
    hidden = jax.nn.gelu(hidden, approximate=False)
    centred = hidden - jnp.mean(hidden, axis=-1, keepdims=True)
    spread = jnp.mean(centred * centred, axis=-1, keepdims=True)
    normed = (centred * lax.rsqrt(spread + 1e-06) * norm_gain + norm_bias).astype(jnp.bfloat16)
    logits = jnp.dot(normed, decoder_weight, preferred_element_type=jnp.float32) + decoder_bias
    activated = jnp.log1p(jnp.maximum(logits, 0.0)).reshape(query_count, query_length, vocab_local)
    live_mask = (token_ids != 0).astype(jnp.float32)[:, :, None]
    columns = term_index * vocab_local + lax.iota(jnp.int32, vocab_local)
    vocab_keep = (columns < VOCAB).astype(jnp.float32)
    weights = (jnp.max(activated * live_mask, axis=1) * vocab_keep).astype(jnp.bfloat16)
    own_hits, own_before = tile_ranks(candidates, tile_total)
    all_weights, all_cand = (
        lax.all_gather(weights, "doc", axis=0, tiled=True),
        lax.all_gather(candidates, "doc", axis=0, tiled=True),
    )
    local_cand = (all_cand - doc_index * tile_local).reshape(doc_count, query_count, cand_count)
    tile_hits, tile_before = tile_ranks(local_cand, tile_local)
    source_row, slot_valid = slot_sources(
        jnp.swapaxes(tile_hits, 1, 2), jnp.swapaxes(tile_before, 1, 2), MOST
    )
    flat_index = lax.iota(jnp.int32, doc_count)[:, None, None] * query_count + source_row
    buffer = jnp.take(all_weights, flat_index.reshape(-1), axis=0).reshape(
        doc_count, tile_local, MOST, vocab_local
    )
    buffer = buffer * slot_valid.astype(jnp.bfloat16)[..., None]
    occupied = occupancy.astype(jnp.bfloat16)
    masked = (
        buffer.reshape(doc_count, tile_local, MOST, blocks_local, block_terms)
        * occupied[None, :, None, :, None]
    )
    partial_value = jnp.einsum(
        "jtrbc,tbdc->jtrd", masked, doc_blocks, preferred_element_type=jnp.float32
    )
    slice_width = tile_docs // term_count
    score_total = lax.psum(partial_value, "term")
    score_share = lax.dynamic_slice_in_dim(score_total, term_index * slice_width, slice_width, 3)
    returned = lax.all_to_all(score_share, "doc", split_axis=0, concat_axis=1, tiled=True)
    slot_rank = jnp.take_along_axis(own_before, candidates, axis=1)
    flat_index = candidates * MOST + slot_rank
    scores = jnp.take(returned.reshape(-1, slice_width), flat_index.reshape(-1), axis=0)
    scores = scores.reshape(query_count, cand_count, slice_width)
    return (weights, scores)


def solution(mesh):
    placed = (
        P("doc", None, None),
        P("doc", None),
        P(),
        P(),
        P(),
        P(),
        P(None, "term"),
        P("term"),
        P("doc", None),
        P("doc", "term"),
        P("doc", "term", None, None),
    )
    return jax.shard_map(
        body,
        mesh=mesh,
        in_specs=placed,
        out_specs=(P("doc", "term"), P("doc", None, "term")),
        check_vma=False,
    )
```

profile of v0, /device:TPU:1, one launch (start us, length us, event | category | flops | bytes accessed | tf_op | source)
XLA Modules:
  0.0 286.4 jit_solution(9171432627118115750)
XLA Ops:
  7.2 0.9 copy.49
  8.2 0.9 copy-done
  9.1 17.5 %fusion.25 = (f32[2048]{0:T(1024)S(1)}, f32[2048,768]{0,1:T(8,128)S(1)}) fusion(f32[768]{0:T(1024)} %param.14, bf16[2048,768]{1,0:T(8,128)(2,1)S(1)} %bitcast.34, bf16[768,768]{1,0:T(8,128)(2,1)} %param.13), kind=kOutput, calls=%fused_computation.67 | convolution fusion | flops 2519726080 | bytes 10628096 | tf_op jit(solution)/shard_map/dot_general | solution.py:50
  26.6 0.7 multiply_reduce_fusion.1
  27.4 1.1 copy-done.4
  28.5 13.7 %multiply_reduce_fusion = f32[64,1920]{1,0:T(8,128)S(1)} fusion(f32[64,32]{1,0:T(8,128)S(1)} %compare_convert_fusion, f32[1920]{0:T(1024)S(1)} %copy-done.5, bf16[768,1920]{1,0:T(8,128)(2,1)S(1)} %copy-done.4, f32[2048,768]{0,1:T(8,128)S(1)} %get-tuple-element.7, f32[768]{0:T(1024)S(1)} %copy-done.6, f32[768]{0:T(1024)S(1)} %copy-done.7, ...), kind=kOutput, calls=%fused_computation.6 | convolution fusion | flops 6063267840 | bytes 9770496 | tf_op jit(solution)/shard_map/dot_general | solution.py:61
  42.2 0.7 multiply_convert_fusion
  43.0 14.4 %all-gather = s32[8,64,32]{1,2,0:T(8,128)S(1)} all-gather(s32[1,64,32]{1,2,0:T(8,128)S(1)} %bitcast.39), channel_id=1, replica_groups=mesh['doc'=8,'term'=16] {'doc'}, dimensions={0}, use_global_device_ids=true | all-gather | bytes 73728 | tf_op jit(solution)/shard_map/all_gather | solution.py:70
  57.4 0.3 convert_reduce_fusion
  57.9 6.6 %fusion.23 = s32[8,16,64]{1,0,2:T(8,128)S(1)} fusion(s32[8,64,16]{2,0,1:T(8,128)S(1)} %copy.56), kind=kOutput, calls=%fused_computation.43 | output fusion | flops 524288 | bytes 65536 | tf_op jit(solution)/shard_map/jit(cumsum)/reduce_window_sum | solution.py:13
  64.6 2.2 select_reduce_fusion
  67.1 2.3 fusion.17
  69.4 2.2 all-gather.3.cloned.1.call-done
  71.6 31.8 %gather_fusion = bf16[4096,1920]{1,0:T(8,128)(2,1)} fusion(bf16[512,1920]{1,0:T(8,128)(2,1)} %all-gather.3.cloned.1.call-done, s32[4096]{0:T(1024)S(1)} %broadcast_clamp_fusion), kind=kCustom, calls=%fused_computation | custom fusion | bytes 31473664 | tf_op jit(solution)/shard_map/jit(_take)/gather | solution.py:78
  103.4 27.2 %gather.18 = bf16[8,16,32,15,128]{4,3,2,1,0:T(8,128)(2,1)} reshape(bf16[4096,1920]{1,0:T(8,128)(2,1)} %gather_fusion) | data formatting | bytes 31457280 | tf_op jit(solution)/shard_map/jit(_take)/gather | solution.py:78
  130.6 14.0 %multiply_multiply_fusion = bf16[8,16,32,15,128]{4,3,2,1,0:T(8,128)(2,1)} fusion(bf16[8,16,32,15,128]{4,3,2,1,0:T(8,128)(2,1)} %gather.18, pred[8,16,32]{2,1,0:T(8,128)(4,1)S(1)} %get-tuple-element.4, bf16[16,15]{1,0:T(8,128)(2,1)S(1)} %convert_element_type.39, bf16[8,16,32]{2,1,0:T(8,128)(2,1)S(1)} %convert_element_type.38), kind=kLoop, calls=%fused_computation.3 | loop fusion | flops 23592960 | bytes 31470048 | tf_op jit(solution)/shard_map/mul | solution.py:84
  144.6 13.5 %fusion.18 = f32[8,16,32,128]{3,2,0,1:T(8,128)} fusion(bf16[16,15,128,128]{3,2,1,0:T(8,128)(2,1)} %param.21, bf16[8,16,32,15,128]{4,3,2,1,0:T(8,128)(2,1)} %multiply_multiply_fusion), kind=kOutput, calls=%fused_computation.39 | convolution fusion | flops 2013265920 | bytes 25690112 | tf_op jit(solution)/shard_map/jtrbc,tbdc->jtrd/dot_general | solution.py:87
  158.2 0.4 convert_reduce_fusion.1
  158.8 13.1 %gather_fusion.2 = s32[2048]{0:T(1024)S(1)} fusion(s32[64,128]{1,0:T(8,128)S(1)} %sub.26, s32[2048]{0:T(1024)S(1)} %reshape.174), kind=kCustom, calls=%fused_computation.2 | custom fusion | bytes 32768 | tf_op jit(solution)/shard_map/jit(take_along_axis)/gather | solution.py:94
  172.1 75.3 %all-reduce.2.cloned.1.call-done = f32[8,16,32,128]{3,2,0,1:T(8,128)} async-done(((f32[8,16,32,128]{3,2,0,1:T(8,128)}), f32[8,16,32,128]{3,2,0,1:T(8,128)}) %all-reduce.2.cloned.1.call-update) | async-done | bytes 2097168 | tf_op jit(solution)/shard_map/psum | solution.py:91
  247.4 2.2 constant_dynamic-slice_fusion
  249.6 0.6 copy.60
  250.2 0.9 reshape.192
  251.1 6.0 %all-to-all-start = ((f32[8,1,4096]{2,1,0:T(1,128)}), f32[8,1,4096]{2,1,0:T(1,128)S(1)}, u32[]{:S(2)}, u32[]{:S(2)}) async-start(f32[8,1,4096]{2,1,0:T(1,128)} %reshape.192), calls=%async_computation | async-start | bytes 262144 | tf_op jit(solution)/shard_map/all_to_all | solution.py:93
  257.1 5.3 %all-to-all-done = f32[8,1,4096]{2,1,0:T(1,128)S(1)} async-done(((f32[8,1,4096]{2,1,0:T(1,128)}), f32[8,1,4096]{2,1,0:T(1,128)S(1)}, u32[]{:S(2)}, u32[]{:S(2)}) %all-to-all-start) | async-done | bytes 131104 | tf_op jit(solution)/shard_map/all_to_all | solution.py:93
  262.4 0.5 broadcast.159
  262.9 1.0 reduce
  263.8 1.0 reshape.193
  264.8 3.2 %copy.66 = f32[8,16,32,8]{3,2,1,0:T(8,128)} copy(f32[8,16,32,8]{2,3,1,0:T(8,128)} %bitcast.38) | data formatting | bytes 262144 | tf_op jit(solution)/shard_map/reshape | solution.py:96
  268.0 9.1 %gather_fusion.1 = f32[2048,8]{1,0:T(8,128)} fusion(f32[4096,8]{1,0:T(8,128)} %bitcast.35, s32[2048]{0:T(1024)S(1)} %broadcast_clamp_fusion.1), kind=kCustom, calls=%fused_computation.1 | custom fusion | bytes 139264 | tf_op jit(solution)/shard_map/jit(_take)/gather | solution.py:96
  277.1 1.8 copy.63
  278.9 0.7 broadcast_select_fusion
  (44 shorter events, 1.3 us)
Async XLA Ops:
  7.2 1.9 copy-start
  7.2 64.4 %all-gather.3.cloned.1.call-start = ((), (), s32[]{:S(2)}) async-start(), calls=%async_computation.1 | async-start | bytes 2211840 | tf_op jit(solution)/shard_map/all_gather | solution.py:69
  26.6 1.8 copy-start.4
  26.6 1.8 copy-start.5
  26.6 1.8 copy-start.6
  26.6 1.8 copy-start.7
  28.4 14.5 %copy-start.3 = (s32[16,15]{1,0:T(8,128)S(1)}, s32[16,15]{1,0:T(8,128)}, u32[]{:S(2)}) copy-start(s32[16,15]{1,0:T(8,128)} %param.20) | copy-start | bytes 2884
  28.4 14.6 %copy-start.2 = (s32[64,32]{0,1:T(8,128)S(1)}, s32[64,32]{0,1:T(8,128)}, u32[]{:S(2)}) copy-start(s32[64,32]{0,1:T(8,128)} %param.19) | copy-start | bytes 24580
  42.9 204.5 %all-reduce.2.cloned.1.call-start = ((), (), s32[]{:S(2)}) async-start(), calls=%async_computation.2 | async-start | bytes 4194304 | tf_op jit(solution)/shard_map/psum | solution.py:91
  251.1 11.2 %all-to-all-start = ((f32[8,1,4096]{2,1,0:T(1,128)}), f32[8,1,4096]{2,1,0:T(1,128)S(1)}, u32[]{:S(2)}, u32[]{:S(2)}) async-start(f32[8,1,4096]{2,1,0:T(1,128)} %reshape.192), calls=%async_computation | async-start | bytes 262144 | tf_op jit(solution)/shard_map/all_to_all | solution.py:93
  264.8 14.8 %copy-start.1 = (bf16[64,32,768]{2,1,0:T(8,128)(2,1)S(1)}, bf16[64,32,768]{2,1,0:T(8,128)(2,1)}, u32[]{:S(2)}) copy-start(bf16[64,32,768]{2,1,0:T(8,128)(2,1)} %param.11) | copy-start | bytes 9437188
Sparse Core Ops, SparseCore 0:
  43.0 28.5 all-gather.2
  158.2 89.1 all-reduce.1
where the time goes:
time: 288 us; the launch traced here: 286 us
  local copies, waits for them, and re-layouts  95 us (33%)
  waiting for transfers between devices  82.8 us (29%)
  matrix products  44.7 us (16%)
  other arithmetic  29.1 us (10%)
  blocking collectives  14.4 us (5%)
  between operations  14.3 us (5%)
  starting transfers between devices  6.05 us (2%)
    psum x1, waiting for transfers between devices, body(): score_total = lax.psum(partial_value, 'term')  75.3 us
    gather x2, local copies, waits for them, and re-layouts, body(): jnp.take(all_weights, flat_index.reshape(-1), axis=0)  59 us
    dot_general x1, matrix products, body(): jnp.dot(query_states.reshape(query_count * query_length, model_width), tr...  17.5 us
    all_gather x1, blocking collectives, body(): lax.all_gather(candidates, 'doc', axis=0, tiled=True)  14.4 us
    mul x1, other arithmetic, body(): buffer.reshape(doc_count, tile_local, MOST, blocks_local, block_terms)  14 us
    dot_general x1, matrix products, body(): jnp.dot(normed, decoder_weight, preferred_element_type=jnp.float32)  13.7 us
    dot_general x1, matrix products, body(): jnp.einsum('jtrbc,tbdc->jtrd', masked, doc_blocks, preferred_element_type...  13.5 us
    gather x3, local copies, waits for them, and re-layouts, body(): slot_rank = jnp.take_along_axis(own_before, candidates, axis=1)  13.2 us
  transfers between devices with their start and end apart: 3, of which 3 were waited for; matrix products, arithmetic and copies ran while one was open for 9% of the time, Pallas kernels for 0%

commit v1 on v0

--- a/solution.py
+++ b/solution.py
@@ -88,7 +88,7 @@
         "jtrbc,tbdc->jtrd", masked, doc_blocks, preferred_element_type=jnp.float32
     )
     slice_width = tile_docs // term_count
-    score_total = lax.psum(partial_value, "term")
+    score_total = jnp.sum(lax.all_gather(partial_value, "term"), axis=0)
     score_share = lax.dynamic_slice_in_dim(score_total, term_index * slice_width, slice_width, 3)
     returned = lax.all_to_all(score_share, "doc", split_axis=0, concat_axis=1, tiled=True)
     slot_rank = jnp.take_along_axis(own_before, candidates, axis=1)

time: 288 us -> 413 us (1.43)
  waiting for transfers between devices: 82.8 us -> 191 us
  other arithmetic: 29.1 us -> 42 us
    all_gather x0 -> x1, waiting for transfers between devices: none -> 183 us  [body(): score_total = jnp.sum(lax.all_gather(partial_value, 'term'), axis=0)]
    psum x1 -> x0, waiting for transfers between devices: 75.3 us -> none  [body(): score_total = lax.psum(partial_value, 'term')]
    reduce_sum x0 -> x1, other arithmetic: none -> 12.9 us  [body(): score_total = jnp.sum(lax.all_gather(partial_value, 'term'), axis=0)]
  transfers between devices with their start and end apart: 3 -> 3, of which waited for: 3 -> 3; matrix products, arithmetic and copies ran while one was open for 9% -> 6% of each run, Pallas kernels for 0% -> 0%
where the time goes in v1:
time: 413 us; the launch traced here: 412 us
  waiting for transfers between devices  191 us (46%)
  local copies, waits for them, and re-layouts  98 us (24%)
  matrix products  47.2 us (11%)
  other arithmetic  42 us (10%)
  blocking collectives  14.4 us (3%)
  between operations  14.3 us (3%)
  starting transfers between devices  5 us (1%)
    all_gather x1, waiting for transfers between devices, body(): score_total = jnp.sum(lax.all_gather(partial_value, 'term'), axis=0)  183 us
    gather x2, local copies, waits for them, and re-layouts, body(): jnp.take(all_weights, flat_index.reshape(-1), axis=0)  59 us
    dot_general x1, matrix products, body(): jnp.dot(query_states.reshape(query_count * query_length, model_width), tr...  17.5 us
    dot_general x1, matrix products, body(): jnp.dot(normed, decoder_weight, preferred_element_type=jnp.float32)  16.3 us
    all_gather x1, blocking collectives, body(): lax.all_gather(candidates, 'doc', axis=0, tiled=True)  14.4 us
    mul x1, other arithmetic, body(): buffer.reshape(doc_count, tile_local, MOST, blocks_local, block_terms)  14 us
    dot_general x1, matrix products, body(): jnp.einsum('jtrbc,tbdc->jtrd', masked, doc_blocks, preferred_element_type...  13.5 us
    gather x3, local copies, waits for them, and re-layouts, body(): slot_rank = jnp.take_along_axis(own_before, candidates, axis=1)  13.2 us
  transfers between devices with their start and end apart: 3, of which 3 were waited for; matrix products, arithmetic and copies ran while one was open for 6% of the time, Pallas kernels for 0%

profile of v1, /device:TPU:1, one launch (start us, length us, event | category | flops | bytes accessed | tf_op | source)
XLA Modules:
  0.0 411.7 jit_solution(5122126522214062323)
XLA Ops:
  7.2 1.8 copy-done
  9.1 17.5 %fusion.25 = (f32[2048]{0:T(1024)S(1)}, f32[2048,768]{0,1:T(8,128)S(1)}) fusion(f32[768]{0:T(1024)} %param.14, bf16[2048,768]{1,0:T(8,128)(2,1)S(1)} %bitcast.35, bf16[768,768]{1,0:T(8,128)(2,1)} %param.13), kind=kOutput, calls=%fused_computation.67 | convolution fusion | flops 2519726080 | bytes 10628096 | tf_op jit(solution)/shard_map/dot_general | solution.py:50
  26.6 2.6 copy-done.2
  29.2 0.7 multiply_reduce_fusion.1
  30.1 16.3 %multiply_reduce_fusion = f32[64,1920]{1,0:T(8,128)S(1)} fusion(f32[64,32]{1,0:T(8,128)S(1)} %compare_convert_fusion, f32[1920]{0:T(1024)S(1)} %copy-done.6, bf16[768,1920]{1,0:T(8,128)(2,1)} %param.17, f32[2048,768]{0,1:T(8,128)} %copy-done.2, f32[768]{0:T(1024)S(1)} %copy-done.7, f32[768]{0:T(1024)S(1)} %copy-done.8, f32[2048]{0:T(1024)S(1)} %add_rsqrt_fusion, ...), kind=kOutput, calls=%fused_computation.6 | convolution fusion | flops 6063267840 | bytes 9770496 | tf_op jit(solution)/shard_map/dot_general | solution.py:61
  46.4 0.7 multiply_convert_fusion
  47.2 14.4 %all-gather.1 = s32[8,64,32]{1,2,0:T(8,128)S(1)} all-gather(s32[1,64,32]{1,2,0:T(8,128)S(1)} %bitcast.41), channel_id=1, replica_groups=mesh['doc'=8,'term'=16] {'doc'}, dimensions={0}, use_global_device_ids=true | all-gather | bytes 73728 | tf_op jit(solution)/shard_map/all_gather | solution.py:70
  61.7 0.3 convert_reduce_fusion
  62.1 6.6 %fusion.23 = s32[8,16,64]{1,0,2:T(8,128)S(1)} fusion(s32[8,64,16]{2,0,1:T(8,128)S(1)} %copy.53), kind=kOutput, calls=%fused_computation.43 | output fusion | flops 524288 | bytes 65536 | tf_op jit(solution)/shard_map/jit(cumsum)/reduce_window_sum | solution.py:13
  68.8 2.2 select_reduce_fusion
  71.3 2.3 fusion.17
  73.6 2.2 all-gather.5.cloned.1.call-done
  75.8 31.8 %gather_fusion = bf16[4096,1920]{1,0:T(8,128)(2,1)} fusion(bf16[512,1920]{1,0:T(8,128)(2,1)} %all-gather.5.cloned.1.call-done, s32[4096]{0:T(1024)S(1)} %broadcast_clamp_fusion), kind=kCustom, calls=%fused_computation | custom fusion | bytes 31473664 | tf_op jit(solution)/shard_map/jit(_take)/gather | solution.py:78
  107.7 27.2 %gather.18 = bf16[8,16,32,15,128]{4,3,2,1,0:T(8,128)(2,1)} reshape(bf16[4096,1920]{1,0:T(8,128)(2,1)} %gather_fusion) | data formatting | bytes 31457280 | tf_op jit(solution)/shard_map/jit(_take)/gather | solution.py:78
  134.8 14.0 %multiply_multiply_fusion = bf16[8,16,32,15,128]{4,3,2,1,0:T(8,128)(2,1)} fusion(bf16[8,16,32,15,128]{4,3,2,1,0:T(8,128)(2,1)} %gather.18, pred[8,16,32]{2,1,0:T(8,128)(4,1)S(1)} %get-tuple-element.4, bf16[16,15]{1,0:T(8,128)(2,1)S(1)} %convert_element_type.39, bf16[8,16,32]{2,1,0:T(8,128)(2,1)S(1)} %convert_element_type.38), kind=kLoop, calls=%fused_computation.3 | loop fusion | flops 23592960 | bytes 31470048 | tf_op jit(solution)/shard_map/mul | solution.py:84
  148.8 13.5 %fusion.18 = f32[8,16,32,128]{3,2,0,1:T(8,128)} fusion(bf16[16,15,128,128]{3,2,1,0:T(8,128)(2,1)} %param.21, bf16[8,16,32,15,128]{4,3,2,1,0:T(8,128)(2,1)} %multiply_multiply_fusion), kind=kOutput, calls=%fused_computation.39 | convolution fusion | flops 2013265920 | bytes 25690112 | tf_op jit(solution)/shard_map/jtrbc,tbdc->jtrd/dot_general | solution.py:87
  162.4 0.4 convert_reduce_fusion.1
  162.9 13.1 %gather_fusion.2 = s32[2048]{0:T(1024)S(1)} fusion(s32[64,128]{1,0:T(8,128)S(1)} %sub.26, s32[2048]{0:T(1024)S(1)} %reshape.174), kind=kCustom, calls=%fused_computation.2 | custom fusion | bytes 32768 | tf_op jit(solution)/shard_map/jit(take_along_axis)/gather | solution.py:94
  176.3 183.1 %all-gather.7.cloned.1.call-done = f32[128,16,32,128]{3,2,0,1:T(8,128)} async-done(((f32[8,16,32,128]{3,2,0,1:T(8,128)}), f32[128,16,32,128]{3,2,0,1:T(8,128)}) %all-gather.7.cloned.1.call-update) | async-done | bytes 33554448 | tf_op jit(solution)/shard_map/all_gather | solution.py:91
  359.5 12.9 %reduce_sum.59 = f32[8,16,32,128]{3,2,0,1:T(8,128)S(1)} reduce(f32[16,8,16,32,128]{4,3,1,0,2:T(8,128)} %bitcast.37, f32[]{:T(128)} %constant.31.clone.1), dimensions={0}, to_apply=%region_9.10 | reduce | flops 7864320 | bytes 35651588 | tf_op jit(solution)/shard_map/reduce_sum | solution.py:91
  372.4 2.0 constant_dynamic-slice_fusion
  374.4 2.2 copy.57
  376.5 0.9 reshape.193
  377.5 4.9 %all-to-all-start = ((f32[8,1,4096]{2,1,0:T(1,128)}), f32[8,1,4096]{2,1,0:T(1,128)S(1)}, u32[]{:S(2)}, u32[]{:S(2)}) async-start(f32[8,1,4096]{2,1,0:T(1,128)} %reshape.193), calls=%async_computation | async-start | bytes 262144 | tf_op jit(solution)/shard_map/all_to_all | solution.py:93
  382.4 5.3 %all-to-all-done = f32[8,1,4096]{2,1,0:T(1,128)S(1)} async-done(((f32[8,1,4096]{2,1,0:T(1,128)}), f32[8,1,4096]{2,1,0:T(1,128)S(1)}, u32[]{:S(2)}, u32[]{:S(2)}) %all-to-all-start) | async-done | bytes 131104 | tf_op jit(solution)/shard_map/all_to_all | solution.py:93
  387.7 0.5 broadcast.159
  388.2 1.0 reduce
  389.1 1.0 reshape.194
  390.1 3.2 copy.58
  393.3 9.1 %gather_fusion.1 = f32[2048,8]{1,0:T(8,128)} fusion(f32[4096,8]{1,0:T(8,128)} %bitcast.36, s32[2048]{0:T(1024)S(1)} %broadcast_clamp_fusion.1), kind=kCustom, calls=%fused_computation.1 | custom fusion | bytes 139264 | tf_op jit(solution)/shard_map/jit(_take)/gather | solution.py:96
  402.4 1.8 copy.59
  404.2 0.7 broadcast_select_fusion
  (47 shorter events, 1.4 us)
Async XLA Ops:
  7.2 1.9 copy-start
  7.2 68.7 %all-gather.5.cloned.1.call-start = ((), (), s32[]{:S(2)}) async-start(), calls=%async_computation.1 | async-start | bytes 2211840 | tf_op jit(solution)/shard_map/all_gather | solution.py:69
  26.6 2.7 copy-start.2
  26.6 3.4 copy-start.4
  26.6 3.5 copy-start.6
  26.6 3.5 copy-start.7
  26.6 3.5 copy-start.8
  30.1 17.1 %copy-start.3 = (s32[64,32]{0,1:T(8,128)S(1)}, s32[64,32]{0,1:T(8,128)}, u32[]{:S(2)}) copy-start(s32[64,32]{0,1:T(8,128)} %param.19) | copy-start | bytes 24580
  30.1 43.5 %copy-start.5 = (s32[16,15]{1,0:T(8,128)S(1)}, s32[16,15]{1,0:T(8,128)}, u32[]{:S(2)}) copy-start(s32[16,15]{1,0:T(8,128)} %param.20) | copy-start | bytes 2884
  47.1 312.3 %all-gather.7.cloned.1.call-start = ((), (), s32[]{:S(2)}) async-start(), calls=%async_computation.2 | async-start | bytes 35651584 | tf_op jit(solution)/shard_map/all_gather | solution.py:91
  377.5 10.2 %all-to-all-start = ((f32[8,1,4096]{2,1,0:T(1,128)}), f32[8,1,4096]{2,1,0:T(1,128)S(1)}, u32[]{:S(2)}, u32[]{:S(2)}) async-start(f32[8,1,4096]{2,1,0:T(1,128)} %reshape.193), calls=%async_computation | async-start | bytes 262144 | tf_op jit(solution)/shard_map/all_to_all | solution.py:93
  390.1 14.8 %copy-start.1 = (bf16[64,32,768]{2,1,0:T(8,128)(2,1)S(1)}, bf16[64,32,768]{2,1,0:T(8,128)(2,1)}, u32[]{:S(2)}) copy-start(bf16[64,32,768]{2,1,0:T(8,128)(2,1)} %param.11) | copy-start | bytes 9437188
Sparse Core Ops, SparseCore 0:
  47.3 28.5 all-gather.4
  162.4 197.0 all-gather.6
